TPU v7x, 32 devices: a whole 2x2x4 slice. The times are simulated.
32 devices in a mesh: group: 4 (over y, x), shard: 8 (over z, core).
Axes of the slice: x: 2, y: 2, z: 4, core: 2. Of those that a mesh axis runs over, the one named last changes fastest.
Arguments:
- queries: bfloat16 [32, 32, 128], P(('group', 'shard')), may hold values from -0.625 to 0.625
- passages: bfloat16 [4096, 128, 128], P(('group', 'shard')), may hold values from -0.5 to 0.5
- lengths: int32 [4096], P(('group', 'shard')), may hold values from 1 to 128
- cand_owner: int32 [32, 1024, 1], P(('group', 'shard')), may hold values from 0 to 31; in each aligned block of 1024 rows (0 to 1023, 1024 to 2047, ..., all dimensions but the last counted through in order) at most 48 rows name the same one
- cand_slot: int32 [32, 1024], P(('group', 'shard')), may hold values from 0 to 127
Outputs:
- scores: float32 [32, 1024], P(('group', 'shard'))
- best_scores: float32 [32, 100], P(('group', 'shard'))
Inputs may be any that keep to these rules, and one draw needn't show every extreme that they name: `cand_owner`: the 1024 candidate rows of one device name any one owner at most 48 times, and some device names some owner exactly 48 times.
All inputs are finite; a program needn't handle non-finite values.
Results may differ from a plain program's by a relative error of at most 0.0003.
Values may be sent and summed in bfloat16 or wider, within the bound.
No kernel may reach another device: no remote copies, remote signals or barrier semaphores. Data moves between devices by JAX's collectives and lax.ppermute only.
A program may use at most 128 MiB of HBM per device.

v0:
```python
import jax
import jax.numpy as jnp
from jax import lax
from jax.sharding import PartitionSpec as P

TOPK = 100


NEGATIVE = -1e30


def maxsim_block(query_rows, pair_codes, passages, lengths):
    passage_count = passages.shape[0]
    present = pair_codes >= 0
    picked = jnp.where(present, pair_codes % passage_count, 0)
    passage_tiles = passages[picked]
    token_limit = lengths[picked]
    similarity = jnp.einsum(
        "sqd,std->sqt", query_rows, passage_tiles, preferred_element_type=jnp.float32
    )
    token_places = lax.broadcasted_iota(jnp.int32, (1, 1, passage_tiles.shape[1]), 2)
    similarity = jnp.where(token_places < token_limit[:, None, None], similarity, NEGATIVE)
    totals = jnp.sum(jnp.max(similarity, axis=2), axis=1)
    return jnp.where(present, totals, 0.0)


def return_scores(group_scores):
    return lax.all_to_all(group_scores, "shard", split_axis=1, concat_axis=1, tiled=True)


def shards(queries, passages, lengths, cand_owner, cand_slot):
    group_total = lax.axis_size("group")
    shard_total = lax.axis_size("shard")
    device_total = group_total * shard_total
    query_local, candidates = cand_slot.shape
    row_total = query_local * candidates
    capacity = 3 * row_total // (2 * device_total)
    passage_total = passages.shape[0]
    owners = cand_owner.reshape(row_total)
    targets = lax.broadcasted_iota(jnp.int32, (1, device_total), 1)
    onehot = (owners[:, None] == targets).astype(jnp.int32)
    earlier = jnp.cumsum(onehot, axis=0) - onehot
    slot_rank = jnp.sum(earlier * onehot, axis=1)
    positions = owners * capacity + slot_rank
    row_query = jnp.arange(row_total, dtype=jnp.int32) // candidates
    pair_codes = row_query * passage_total + cand_slot.reshape(row_total)
    send_codes = jnp.full((device_total * capacity,), -1, jnp.int32).at[positions].set(pair_codes)
    send_codes = send_codes.reshape(group_total, shard_total, capacity)
    everyone = lax.all_gather(queries, ("group", "shard"), axis=0, tiled=True)
    moved_codes_all = lax.all_to_all(send_codes, "group", split_axis=0, concat_axis=0, tiled=True)
    moved_codes = lax.all_to_all(moved_codes_all, "shard", split_axis=1, concat_axis=1, tiled=True)
    item_total = moved_codes.shape[2]
    flat_codes = moved_codes.reshape(group_total, shard_total * item_total)
    source_shard = lax.broadcasted_iota(jnp.int32, (shard_total, item_total), 0).reshape(
        shard_total * item_total
    )

    def one_group(packed):
        group_codes, group_index = packed
        source_device = group_index * shard_total + source_shard
        query_index = source_device * query_local + jnp.maximum(group_codes, 0) // passage_total
        return maxsim_block(everyone[query_index], group_codes, passages, lengths)

    group_scores = lax.map(one_group, (flat_codes, jnp.arange(group_total, dtype=jnp.int32)))
    returned = return_scores(group_scores.reshape(group_total, shard_total, item_total))
    home_scores = lax.all_to_all(returned, "group", split_axis=0, concat_axis=0, tiled=True)
    scores = home_scores.reshape(device_total * capacity)[positions].reshape(
        query_local, candidates
    )
    best_scores = lax.top_k(scores, TOPK)[0]
    return (scores, best_scores)


def solution(mesh):
    placed = (
        P(("group", "shard"), None, None),
        P(("group", "shard"), None, None),
        P(("group", "shard")),
        P(("group", "shard"), None, None),
        P(("group", "shard"), None),
    )
    return jax.shard_map(
        shards,
        mesh=mesh,
        in_specs=placed,
        out_specs=(P(("group", "shard"), None), P(("group", "shard"), None)),
        check_vma=False,
    )
```

profile of v0, /device:TPU:0, one launch (start us, length us, event | category | flops | bytes accessed | tf_op | source)
XLA Modules:
  0.0 231.5 jit_solution(5603280642094741370)
XLA Ops:
  0.6 0.7 fusion.8
  1.3 9.0 %reduce-window.6 = s32[32,8,128]{2,1,0:T(8,128)S(1)} reduce-window(s32[32,8,128]{2,1,0:T(8,128)S(1)} %fusion.8, s32[]{:T(128)} %constant.118.clone.1), window={size=1x1x128 pad=0_0x0_0x127_0}, to_apply=%region_0.0 | reduce-window | flops 4161536 | bytes 262148 | tf_op jit(solution)/shard_map/reduce-window
  10.4 0.1 copy.30
  10.8 0.7 fusion.7
  11.5 0.7 compare_select_fusion.6
  12.2 0.7 fusion.10
  12.9 4.3 %scatter_custom_fusion = s32[1536]{0:T(1024)S(1)} fusion(s32[1024]{0:T(1024)S(1)} %bitcast.61, s32[1024]{0:T(1024)S(1)} %fusion.10, s32[]{:T(128)} %constant.120.clone.1), kind=kCustom, calls=%fused_computation.42 | custom fusion | bytes 6148 | tf_op jit(solution)/shard_map/scatter | solution.py:47
  17.4 9.7 %all_to_all.20 = s32[4,1,384]{2,1,0:T(1,128)S(1)} all-to-all(s32[4,1,384]{2,1,0:T(1,128)S(1)} %reshape.292), channel_id=1, replica_groups=mesh['group'=4,'shard'=8] {'group'}, dimensions={0} | all-to-all | bytes 12288 | tf_op jit(solution)/shard_map/all_to_all | solution.py:50
  27.1 0.5 broadcast.314
  27.6 0.7 reduce.4
  28.4 0.7 reshape.294
  29.1 4.9 %all-to-all-start.1 = ((s32[8,1,192]{2,1,0:T(1,128)}), s32[8,1,192]{2,1,0:T(1,128)S(1)}, u32[]{:S(2)}, u32[]{:S(2)}) async-start(s32[8,1,192]{2,1,0:T(1,128)} %reshape.294), calls=%async_computation.1 | async-start | bytes 16384 | tf_op jit(solution)/shard_map/all_to_all | solution.py:51
  33.9 41.4 %all_gather.3 = bf16[32,32,128]{2,1,0:T(8,128)(2,1)S(1)} all-gather(bf16[1,32,128]{2,1,0:T(8,128)(2,1)} %param.7), channel_id=1, replica_groups=mesh['group'=4,'shard'=8] {'group','shard'}, dimensions={0}, use_global_device_ids=true | all-gather | bytes 270336 | tf_op jit(solution)/shard_map/all_gather | solution.py:49
  75.3 0.7 reduce.5
  76.1 126.1 %while.13 = (s32[]{:T(128)}, f32[4,384]{1,0:T(4,128)S(1)}, s32[4,384]{1,0:T(4,128)S(1)}, s32[128]{0:T(128)}, s32[4]{0:T(128)S(1)}, /*index=5*/bf16[32,32,128]{2,...) while((s32[]{:T(128)}, f32[4,384]{1,0:T(4,128)S(1)}, ...), condition=%wide.region_7.8_spmd.clone, body=%wide.region_4.7_spmd.clone.sunk | while | flops 405862016 | bytes 47428276 | solution.py:64
  76.2 0.6 dynamic_slice.28
  77.6 13.3 %gather_fusion.2 = bf16[384,128,128]{2,1,0:T(8,128)(2,1)} fusion(bf16[128,128,128]{2,1,0:T(8,128)(2,1)} %get-tuple-element.224, s32[1024]{0:T(1024)S(1)} %get-tuple-element.194), kind=kCustom, calls=%fused_computation.2.clone.clone.1 | custom fusion | bytes 25167360 | tf_op jit(solution)/shard_map/while/body/eval_jaxpr/gather | solution.py:16
  90.9 2.7 %gather_fusion = s32[384]{0:T(512)S(1)} fusion(s32[128]{0:T(128)S(1)} %copy-done, s32[1024]{0:T(1024)S(1)} %get-tuple-element.194), kind=kCustom, calls=%fused_computation.clone.clone.1 | custom fusion | bytes 4608 | tf_op jit(solution)/shard_map/while/body/eval_jaxpr/gather | solution.py:17
  93.7 2.4 %gather_fusion.1 = bf16[384,32,128]{2,1,0:T(8,128)(2,1)S(1)} fusion(bf16[32,32,128]{2,1,0:T(8,128)(2,1)S(1)} %get-tuple-element.223, s32[1024]{0:T(1024)S(1)} %get-tuple-element.195), kind=kCustom, calls=%fused_computation.1.clone.clone.1 | custom fusion | bytes 6292992 | tf_op jit(solution)/shard_map/while/body/eval_jaxpr/gather | solution.py:62
  96.1 10.4 %select_reduce_fusion.2 = f32[384,32]{1,0:T(8,128)} fusion(pred[384,128]{1,0:T(8,128)(4,1)S(1)} %iota_compare_fusion.4, bf16[384,32,128]{2,1,0:T(8,128)(2,1)S(1)} %gather_fusion.1, bf16[384,128,128]{2,1,0:T(8,128)(2,1)} %gather_fusion.2), kind=kOutput, calls=%fused_computation.6.clone.1 | convolution fusion | flops 405786624 | bytes 15826944 | tf_op jit(solution)/shard_map/while/body/eval_jaxpr/sqd,std->sqt/dot_general | solution.py:18
  106.6 1.1 reduce_sum.34
  107.7 0.6 dynamic_slice.28
  109.1 13.2 %gather_fusion.2 = bf16[384,128,128]{2,1,0:T(8,128)(2,1)} fusion(bf16[128,128,128]{2,1,0:T(8,128)(2,1)} %get-tuple-element.224, s32[1024]{0:T(1024)S(1)} %get-tuple-element.194), kind=kCustom, calls=%fused_computation.2.clone.clone.1 | custom fusion | bytes 25167360 | tf_op jit(solution)/shard_map/while/body/eval_jaxpr/gather | solution.py:16
  122.3 2.7 %gather_fusion = s32[384]{0:T(512)S(1)} fusion(s32[128]{0:T(128)S(1)} %copy-done, s32[1024]{0:T(1024)S(1)} %get-tuple-element.194), kind=kCustom, calls=%fused_computation.clone.clone.1 | custom fusion | bytes 4608 | tf_op jit(solution)/shard_map/while/body/eval_jaxpr/gather | solution.py:17
  125.1 2.4 %gather_fusion.1 = bf16[384,32,128]{2,1,0:T(8,128)(2,1)S(1)} fusion(bf16[32,32,128]{2,1,0:T(8,128)(2,1)S(1)} %get-tuple-element.223, s32[1024]{0:T(1024)S(1)} %get-tuple-element.195), kind=kCustom, calls=%fused_computation.1.clone.clone.1 | custom fusion | bytes 6292992 | tf_op jit(solution)/shard_map/while/body/eval_jaxpr/gather | solution.py:62
  127.6 10.4 %select_reduce_fusion.2 = f32[384,32]{1,0:T(8,128)} fusion(pred[384,128]{1,0:T(8,128)(4,1)S(1)} %iota_compare_fusion.4, bf16[384,32,128]{2,1,0:T(8,128)(2,1)S(1)} %gather_fusion.1, bf16[384,128,128]{2,1,0:T(8,128)(2,1)} %gather_fusion.2), kind=kOutput, calls=%fused_computation.6.clone.1 | convolution fusion | flops 405786624 | bytes 15826944 | tf_op jit(solution)/shard_map/while/body/eval_jaxpr/sqd,std->sqt/dot_general | solution.py:18
  138.0 1.1 reduce_sum.34
  139.2 0.6 dynamic_slice.28
  140.6 13.3 %gather_fusion.2 = bf16[384,128,128]{2,1,0:T(8,128)(2,1)} fusion(bf16[128,128,128]{2,1,0:T(8,128)(2,1)} %get-tuple-element.224, s32[1024]{0:T(1024)S(1)} %get-tuple-element.194), kind=kCustom, calls=%fused_computation.2.clone.clone.1 | custom fusion | bytes 25167360 | tf_op jit(solution)/shard_map/while/body/eval_jaxpr/gather | solution.py:16
  153.9 2.7 %gather_fusion = s32[384]{0:T(512)S(1)} fusion(s32[128]{0:T(128)S(1)} %copy-done, s32[1024]{0:T(1024)S(1)} %get-tuple-element.194), kind=kCustom, calls=%fused_computation.clone.clone.1 | custom fusion | bytes 4608 | tf_op jit(solution)/shard_map/while/body/eval_jaxpr/gather | solution.py:17
  156.7 2.4 %gather_fusion.1 = bf16[384,32,128]{2,1,0:T(8,128)(2,1)S(1)} fusion(bf16[32,32,128]{2,1,0:T(8,128)(2,1)S(1)} %get-tuple-element.223, s32[1024]{0:T(1024)S(1)} %get-tuple-element.195), kind=kCustom, calls=%fused_computation.1.clone.clone.1 | custom fusion | bytes 6292992 | tf_op jit(solution)/shard_map/while/body/eval_jaxpr/gather | solution.py:62
  159.1 10.4 %select_reduce_fusion.2 = f32[384,32]{1,0:T(8,128)} fusion(pred[384,128]{1,0:T(8,128)(4,1)S(1)} %iota_compare_fusion.4, bf16[384,32,128]{2,1,0:T(8,128)(2,1)S(1)} %gather_fusion.1, bf16[384,128,128]{2,1,0:T(8,128)(2,1)} %gather_fusion.2), kind=kOutput, calls=%fused_computation.6.clone.1 | convolution fusion | flops 405786624 | bytes 15826944 | tf_op jit(solution)/shard_map/while/body/eval_jaxpr/sqd,std->sqt/dot_general | solution.py:18
  169.6 1.1 reduce_sum.34
  170.7 0.6 dynamic_slice.28
  172.1 13.3 %gather_fusion.2 = bf16[384,128,128]{2,1,0:T(8,128)(2,1)} fusion(bf16[128,128,128]{2,1,0:T(8,128)(2,1)} %get-tuple-element.224, s32[1024]{0:T(1024)S(1)} %get-tuple-element.194), kind=kCustom, calls=%fused_computation.2.clone.clone.1 | custom fusion | bytes 25167360 | tf_op jit(solution)/shard_map/while/body/eval_jaxpr/gather | solution.py:16
  185.4 2.7 %gather_fusion = s32[384]{0:T(512)S(1)} fusion(s32[128]{0:T(128)S(1)} %copy-done, s32[1024]{0:T(1024)S(1)} %get-tuple-element.194), kind=kCustom, calls=%fused_computation.clone.clone.1 | custom fusion | bytes 4608 | tf_op jit(solution)/shard_map/while/body/eval_jaxpr/gather | solution.py:17
  188.2 2.4 %gather_fusion.1 = bf16[384,32,128]{2,1,0:T(8,128)(2,1)S(1)} fusion(bf16[32,32,128]{2,1,0:T(8,128)(2,1)S(1)} %get-tuple-element.223, s32[1024]{0:T(1024)S(1)} %get-tuple-element.195), kind=kCustom, calls=%fused_computation.1.clone.clone.1 | custom fusion | bytes 6292992 | tf_op jit(solution)/shard_map/while/body/eval_jaxpr/gather | solution.py:62
  190.7 10.4 %select_reduce_fusion.2 = f32[384,32]{1,0:T(8,128)} fusion(pred[384,128]{1,0:T(8,128)(4,1)S(1)} %iota_compare_fusion.4, bf16[384,32,128]{2,1,0:T(8,128)(2,1)S(1)} %gather_fusion.1, bf16[384,128,128]{2,1,0:T(8,128)(2,1)} %gather_fusion.2), kind=kOutput, calls=%fused_computation.6.clone.1 | convolution fusion | flops 405786624 | bytes 15826944 | tf_op jit(solution)/shard_map/while/body/eval_jaxpr/sqd,std->sqt/dot_general | solution.py:18
  201.1 1.1 reduce_sum.34
  202.4 8.0 %all_to_all.21 = f32[8,1,192]{2,1,0:T(1,128)S(1)} all-to-all(f32[8,1,192]{2,1,0:T(1,128)S(1)} %reshape.296), channel_id=1, replica_groups=mesh['group'=4,'shard'=8] {'shard'}, dimensions={0} | all-to-all | bytes 12288 | tf_op jit(solution)/shard_map/all_to_all | solution.py:28
  210.4 0.5 broadcast.316
  210.9 0.7 reduce.6
  211.7 0.7 reshape.298
  212.3 3.2 %all-to-all-start.3 = ((f32[4,1,384]{2,1,0:T(1,128)}), f32[4,1,384]{2,1,0:T(1,128)S(1)}, u32[]{:S(2)}, u32[]{:S(2)}) async-start(f32[4,1,384]{2,1,0:T(1,128)} %reshape.298), calls=%async_computation.3 | async-start | bytes 12288 | tf_op jit(solution)/shard_map/all_to_all | solution.py:66
  215.6 4.6 %all-to-all-done.3 = f32[4,1,384]{2,1,0:T(1,128)S(1)} async-done(((f32[4,1,384]{2,1,0:T(1,128)}), f32[4,1,384]{2,1,0:T(1,128)S(1)}, u32[]{:S(2)}, u32[]{:S(2)}) %all-to-all-start.3) | async-done | bytes 6176 | tf_op jit(solution)/shard_map/all_to_all | solution.py:66
  220.3 0.7 reduce.7
  221.1 6.2 %gather_fusion.3 = f32[1024]{0:T(1024)S(1)} fusion(f32[1536]{0:T(1024)S(1)} %reshape.234, s32[1024]{0:T(1024)S(1)} %broadcast_clamp_fusion), kind=kCustom, calls=%fused_computation.3 | custom fusion | bytes 12288 | tf_op jit(solution)/shard_map/gather | solution.py:67
  227.3 4.2 %sort_prefixfusion = f32[1,100]{1,0:T(1,128)} fusion(f32[1,1024]{1,0:T(1,128)S(1)} %bitcast.63), kind=kCustom, calls=%top_k.9.sort_prefix | custom fusion | flops 10240 | bytes 4496 | tf_op jit(solution)/shard_map/top_k | solution.py:70
  (65 shorter events, 2.4 us)
Async XLA Ops:
  29.1 46.2 %all-to-all-start.1 = ((s32[8,1,192]{2,1,0:T(1,128)}), s32[8,1,192]{2,1,0:T(1,128)S(1)}, u32[]{:S(2)}, u32[]{:S(2)}) async-start(s32[8,1,192]{2,1,0:T(1,128)} %reshape.294), calls=%async_computation.1 | async-start | bytes 16384 | tf_op jit(solution)/shard_map/all_to_all | solution.py:51
  77.5 13.3 %copy-start = (s32[128]{0:T(128)S(1)}, s32[128]{0:T(128)}, u32[]{:S(2)}) copy-start(s32[128]{0:T(128)} %get-tuple-element.221) | copy-start | bytes 1540 | tf_op jit(solution)/shard_map/while
  109.1 13.2 %copy-start = (s32[128]{0:T(128)S(1)}, s32[128]{0:T(128)}, u32[]{:S(2)}) copy-start(s32[128]{0:T(128)} %get-tuple-element.221) | copy-start | bytes 1540 | tf_op jit(solution)/shard_map/while
  140.5 13.3 %copy-start = (s32[128]{0:T(128)S(1)}, s32[128]{0:T(128)}, u32[]{:S(2)}) copy-start(s32[128]{0:T(128)} %get-tuple-element.221) | copy-start | bytes 1540 | tf_op jit(solution)/shard_map/while
  172.1 13.3 %copy-start = (s32[128]{0:T(128)S(1)}, s32[128]{0:T(128)}, u32[]{:S(2)}) copy-start(s32[128]{0:T(128)} %get-tuple-element.221) | copy-start | bytes 1540 | tf_op jit(solution)/shard_map/while
  212.3 7.9 %all-to-all-start.3 = ((f32[4,1,384]{2,1,0:T(1,128)}), f32[4,1,384]{2,1,0:T(1,128)S(1)}, u32[]{:S(2)}, u32[]{:S(2)}) async-start(f32[4,1,384]{2,1,0:T(1,128)} %reshape.298), calls=%async_computation.3 | async-start | bytes 12288 | tf_op jit(solution)/shard_map/all_to_all | solution.py:66
  227.2 4.3 %copy-start.1 = (f32[1024]{0:T(1024)}, f32[1024]{0:T(1024)S(1)}, u32[]{:S(2)}) copy-start(f32[1024]{0:T(1024)S(1)} %gather_fusion.3) | copy-start | bytes 12292
where the time goes:
time: 232 us
  local copies, waits for them, and re-layouts  90.5 us (39%)
  blocking collectives  59 us (25%)
  matrix products  41.7 us (18%)
  other arithmetic  23.9 us (10%)
  starting transfers between devices  8.12 us (3%)
  waiting for transfers between devices  4.64 us (2%)
  loops' own time  2.87 us (1%)
    gather x4, local copies, waits for them, and re-layouts, maxsim_block(): passage_tiles = passages[picked]  53.1 us
    dot_general x4, matrix products, maxsim_block(): jnp.einsum('sqd,std->sqt', query_rows, passage_tiles, preferred_element_t...  41.7 us
    all_gather x1, blocking collectives, shards(): everyone = lax.all_gather(queries, ('group', 'shard'), axis=0, tiled=True)  41.4 us
    gather x4, local copies, waits for them, and re-layouts, maxsim_block(): token_limit = lengths[picked]  10.7 us
    gather x4, local copies, waits for them, and re-layouts, one_group(): return maxsim_block(everyone[query_index], group_codes, passages, lengths)  9.77 us
    all_to_all x1, blocking collectives, shards(): lax.all_to_all(send_codes, 'group', split_axis=0, concat_axis=0, tiled=True)  9.68 us
    another operation x3, other arithmetic  9.15 us
    all_to_all x1, blocking collectives, return_scores(): lax.all_to_all(group_scores, 'shard', split_axis=1, concat_axis=1, tiled=...  7.97 us
  transfers between devices with their start and end apart: 2, of which 1 were waited for; matrix products, arithmetic and copies ran while one was open for 0% of the time, Pallas kernels for 0%

commit v1 on v0

v1 whole, which is shorter than its diff:
```python
import jax
import jax.numpy as jnp
from jax import lax
from jax.experimental import pallas as pl
from jax.experimental.pallas import tpu as pltpu
from jax.sharding import PartitionSpec as P

TOPK = 100
NEGATIVE = -1e30
LANES = 128
AXES = ("group", "shard")


def score_body(lengths_ref, passages_ref, queries_ref, scores_ref, transposed_ref, best_ref):
    step = pl.program_id(1)
    query_count, query_tokens, depth = queries_ref.shape
    block, passage_tokens, _ = passages_ref.shape
    columns = query_count * query_tokens

    @pl.when(step == 0)
    def _():
        transposed_ref[...] = queries_ref[...].reshape(columns, depth).T

    rows = passages_ref[...].reshape(block * passage_tokens, depth)
    width = min(256, columns)
    for start in range(0, columns, width):
        similarity = jnp.dot(
            rows, transposed_ref[:, start : start + width], preferred_element_type=jnp.float32
        ).reshape(block, passage_tokens, width)
        token = lax.broadcasted_iota(jnp.int32, (passage_tokens, width), 0)
        for j in range(block):
            limited = jnp.where(token < lengths_ref[step * block + j], similarity[j], NEGATIVE)
            best_ref[pl.ds(step * block + j, 1), start : start + width] = jnp.max(
                limited, axis=0, keepdims=True
            )

    @pl.when(step == pl.num_programs(1) - 1)
    def _():
        query = lax.broadcasted_iota(jnp.int32, (query_count, columns), 0)
        column = lax.broadcasted_iota(jnp.int32, (query_count, columns), 1)
        first = query * query_tokens
        mine = ((column >= first) & (column < first + query_tokens)).astype(jnp.float32)
        scores_ref[...] = lax.dot_general(
            mine,
            best_ref[...],
            (((1,), (1,)), ((), ())),
            precision=lax.Precision.HIGHEST,
            preferred_element_type=jnp.float32,
        )


def score_all(queries, passages, lengths):
    query_total, query_tokens, depth = queries.shape
    passage_total, passage_tokens, _ = passages.shape
    tile = min(query_total, 32)
    block = min(passage_total, 16)
    columns = tile * query_tokens
    return pl.pallas_call(
        score_body,
        out_shape=jax.ShapeDtypeStruct((query_total, passage_total), jnp.float32),
        grid_spec=pltpu.PrefetchScalarGridSpec(
            num_scalar_prefetch=1,
            grid=(query_total // tile, passage_total // block),
            in_specs=[
                pl.BlockSpec((block, passage_tokens, depth), lambda q, i, _: (i, 0, 0)),
                pl.BlockSpec((tile, query_tokens, depth), lambda q, i, _: (q, 0, 0)),
            ],
            out_specs=pl.BlockSpec((tile, passage_total), lambda q, i, _: (q, 0)),
            scratch_shapes=[
                pltpu.VMEM((depth, columns), jnp.bfloat16),
                pltpu.VMEM((passage_total, columns), jnp.float32),
            ],
        ),
        name="maxsim",
    )(lengths, passages, queries)


def pick_body(table_ref, owner_ref, slot_ref, scores_ref, best_ref):
    owners, passages = table_ref.shape
    chunks = owner_ref.shape[1] // LANES

    def grid_of(ref):
        return jnp.concatenate(
            [ref[:, r * LANES : (r + 1) * LANES] for r in range(chunks)], axis=0
        )

    owner = grid_of(owner_ref)
    slot = grid_of(slot_ref)
    picked = jnp.zeros(owner.shape, jnp.float32)
    for o in range(owners):
        row = jnp.broadcast_to(table_ref[o : o + 1, :], owner.shape[:1] + (passages,))
        picked = jnp.where(owner == o, jnp.take_along_axis(row, slot, axis=1), picked)
    for r in range(chunks):
        scores_ref[:, r * LANES : (r + 1) * LANES] = picked[r : r + 1]

    square = (LANES, LANES)
    lower = lax.broadcasted_iota(jnp.int32, square, 0) < lax.broadcasted_iota(jnp.int32, square, 1)
    along = [jnp.broadcast_to(picked[r : r + 1], square) for r in range(chunks)]
    down = [a.T for a in along]
    place = lax.broadcasted_iota(jnp.int32, square, 0)
    kept = jnp.zeros(square, jnp.float32)
    for i in range(chunks):
        ahead = jnp.zeros(square, jnp.int32)
        for j in range(chunks):
            if j < i:
                wins = down[j] >= along[i]
            elif j > i:
                wins = down[j] > along[i]
            else:
                wins = (down[j] > along[i]) | ((down[j] == along[i]) & lower)
            ahead = ahead + wins.astype(jnp.int32)
        rank = jnp.sum(ahead, axis=0, keepdims=True)
        kept = kept + jnp.where(place == rank, along[i], 0.0)
    best_ref[...] = jnp.sum(kept.T, axis=0, keepdims=True)[:, : best_ref.shape[1]]


def pick(table, owner, slot):
    rows, candidates = slot.shape
    return pl.pallas_call(
        pick_body,
        out_shape=(
            jax.ShapeDtypeStruct((rows, candidates), jnp.float32),
            jax.ShapeDtypeStruct((rows, TOPK), jnp.float32),
        ),
        name="pick",
    )(table, owner, slot)


def shards(queries, passages, lengths, cand_owner, cand_slot):
    device_total = lax.axis_size("group") * lax.axis_size("shard")
    query_local, candidates = cand_slot.shape
    sent = jnp.broadcast_to(queries, (device_total,) + queries.shape[1:])
    everyone = lax.all_to_all(sent, AXES, split_axis=0, concat_axis=0, tiled=True)
    scores = score_all(everyone, passages, lengths)
    table = lax.all_to_all(scores, AXES, split_axis=0, concat_axis=0, tiled=True)
    return pick(table, cand_owner.reshape(query_local, candidates), cand_slot)


def solution(mesh):
    placed = (
        P(AXES, None, None),
        P(AXES, None, None),
        P(AXES),
        P(AXES, None, None),
        P(AXES, None),
    )
    return jax.shard_map(
        shards,
        mesh=mesh,
        in_specs=placed,
        out_specs=(P(AXES, None), P(AXES, None)),
        check_vma=False,
    )
```

time: 232 us -> 44.6 us (0.19)
  local copies, waits for them, and re-layouts: 90.5 us -> 0.73 us
  matrix products: 41.7 us -> 0 us
  blocking collectives: 59 us -> 27.5 us
  other arithmetic: 23.9 us -> 0 us
  Pallas kernels: 0 us -> 15.5 us
  starting transfers between devices: 8.12 us -> 0 us
  waiting for transfers between devices: 4.64 us -> 0 us
  loops' own time: 2.87 us -> 0 us
    gather x13 -> x0, local copies, waits for them, and re-layouts: 79.7 us -> none  [the longest x4 53.1 us: maxsim_block(): passage_tiles = passages[picked]]
    dot_general x4 -> x0, matrix products: 41.7 us -> none  [maxsim_block(): jnp.einsum('sqd,std->sqt', query_rows, passage_tiles, preferred_element_t...]
    all_gather x1 -> x0, blocking collectives: 41.4 us -> none  [shards(): everyone = lax.all_gather(queries, ('group', 'shard'), axis=0, tiled=True)]
    pallas_call x0 -> x2, Pallas kernels: none -> 15.5 us  [the longest x1 13.5 us: score_all(): pl.pallas_call(score_body, out_shape=jax.ShapeDtypeStruct((query_total, p...]
    all_to_all x2, blocking collectives: 17.7 us -> 27.5 us  [the longest x1 17.2 us: shards(): lax.all_to_all(sent, AXES, split_axis=0, concat_axis=0, tiled=True)]
    another operation x3 -> x0, other arithmetic: 9.15 us -> none
    all_to_all x2 -> x0, starting transfers between devices: 8.12 us -> none  [the longest x1 4.88 us: shards(): lax.all_to_all(moved_codes_all, 'shard', split_axis=1, concat_axis=1, til...]
    reduce_sum x5 -> x0, other arithmetic: 4.99 us -> none  [the longest x4 4.27 us: maxsim_block(): totals = jnp.sum(jnp.max(similarity, axis=2), axis=1)]
  transfers between devices with their start and end apart: 2 -> 0, of which waited for: 1 -> 0; matrix products, arithmetic and copies ran while one was open for 0% -> 0% of each run, Pallas kernels for 0% -> 0%
where the time goes in v1:
time: 44.6 us; the launch traced here: 44.3 us
  blocking collectives  27.5 us (62%)
  Pallas kernels  15.5 us (35%)
  local copies, waits for them, and re-layouts  0.73 us (2%)
  between operations  0.63 us (1%)
    all_to_all x1, blocking collectives, shards(): lax.all_to_all(sent, AXES, split_axis=0, concat_axis=0, tiled=True)  17.2 us
    pallas_call x1, Pallas kernels, score_all(): pl.pallas_call(score_body, out_shape=jax.ShapeDtypeStruct((query_total, p...  13.5 us
    all_to_all x1, blocking collectives, shards(): lax.all_to_all(scores, AXES, split_axis=0, concat_axis=0, tiled=True)  10.3 us
    pallas_call x1, Pallas kernels, pick(): pl.pallas_call(pick_body, out_shape=(jax.ShapeDtypeStruct((rows, candidat...  2.01 us

profile of v1, /device:TPU:0, one launch (start us, length us, event | category | flops | bytes accessed | tf_op | source)
XLA Modules:
  0.0 44.3 jit_solution(2434561211037874409)
XLA Ops:
  0.6 0.7 %broadcast_in_dim.8 = bf16[32,32,128]{2,1,0:T(8,128)(2,1)S(1)} broadcast(bf16[32,128]{1,0:T(8,128)(2,1)} %bitcast.8), dimensions={1,2} | broadcast | bytes 270336 | tf_op jit(solution)/shard_map/broadcast_in_dim | solution.py:132
  1.4 17.2 %all_to_all.16.queries_ref = bf16[32,32,128]{2,1,0:T(8,128)(2,1)} all-to-all(bf16[32,32,128]{2,1,0:T(8,128)(2,1)S(1)} %broadcast_in_dim.8), channel_id=1, replica_groups=mesh['group'=4,'shard'=8] {'group','shard'}, dimensions={0} | all-to-all | bytes 524288 | tf_op jit(solution)/shard_map/all_to_all | solution.py:133
  18.6 13.5 %maxsim.1 = f32[32,128]{1,0:T(8,128)} custom-call(s32[128]{0:T(128)} %lengths_ref.1, bf16[128,128,128]{2,1,0:T(8,128)(2,1)} %passages_ref.1, bf16[32,32,128]{2,1,0:T(8,128)(2,1)} %all_to_all.16.queries_ref), custom_call_target="tpu_custom_call" | custom-call | tf_op jit(solution)/shard_map/maxsim/pallas_call | solution.py:58
  32.1 10.3 %all_to_all.17 = f32[32,1,128]{2,1,0:T(1,128)} all-to-all(f32[32,1,128]{2,1,0:T(1,128)} %bitcast.6), channel_id=1, replica_groups=mesh['group'=4,'shard'=8] {'group','shard'}, dimensions={0} | all-to-all | bytes 32768 | tf_op jit(solution)/shard_map/all_to_all | solution.py:135
  42.3 2.0 %pick.1 = (f32[1,1024]{1,0:T(1,128)}, f32[1,100]{1,0:T(1,128)}) custom-call(f32[32,128]{1,0:T(8,128)} %bitcast.7, s32[1,1024]{1,0:T(1,128)} %bitcast.9, s32[1,1024]{1,0:T(1,128)} %slot_ref.1), custom_call_target="tpu_custom_call" | custom-call | tf_op jit(solution)/shard_map/pick/pallas_call | solution.py:119

commit v2 on v1

v2 whole, which is shorter than its diff:
```python
import functools

import jax
import jax.numpy as jnp
from jax import lax
from jax.experimental import pallas as pl
from jax.experimental.pallas import tpu as pltpu
from jax.sharding import PartitionSpec as P

TOPK = 100
NEGATIVE = -1e30
LANES = 128
SUBLANES = 8
PITCH = SUBLANES + 1
CHUNK = 16
BLOCK = 64
KERNEL_VMEM = 24 << 20
AXES = ("group", "shard")
WHOLE = pl.BlockSpec(memory_space=pltpu.VMEM)
SCALARS = pl.BlockSpec(memory_space=pltpu.SMEM)


def pack_body(
    lengths_ref, passages_ref, near_ref, far_ref, codes_ref, total_ref, packed_ref, sem
):
    passage_total, passage_tokens, depth = passages_ref.shape
    most = passage_tokens // CHUNK

    def place(p, at):
        length = lengths_ref[p]
        count = lax.div(length + (CHUNK - 1), CHUNK)
        last = count - 1
        packed_ref[pl.ds(at, most)] = passages_ref[p].reshape(most, CHUNK, depth)
        first_token = passages_ref[p, 0:CHUNK].astype(jnp.float32)[0:1]
        tail = passages_ref[p, pl.ds(pl.multiple_of(last * CHUNK, CHUNK), CHUNK)]
        row = lax.broadcasted_iota(jnp.int32, (CHUNK, depth), 0)
        filled = jnp.where(row < length - last * CHUNK, tail.astype(jnp.float32), first_token)
        packed_ref[pl.ds(at + last, 1)] = filled.astype(packed_ref.dtype)[None]
        codes_ref[at] = 2 * p + 1
        for k in range(1, most):
            codes_ref[at + k] = 2 * p
        return at + count

    total = lax.fori_loop(0, passage_total, place, jnp.int32(0), unroll=4)
    total_ref[0] = total
    near = near_ref.shape[0]
    copies = [
        pltpu.make_async_copy(packed_ref.at[pl.ds(0, near)], near_ref, sem.at[0]),
        pltpu.make_async_copy(packed_ref.at[pl.ds(near, far_ref.shape[0])], far_ref, sem.at[1]),
    ]
    for copy in copies:
        copy.start()

    def fill(k, carry):
        codes_ref[total + k] = 2 * passage_total + 1
        return carry

    lax.fori_loop(0, codes_ref.shape[0] - passage_total * most, fill, 0, unroll=8)
    for copy in copies:
        copy.wait()


def pack(passages, lengths):
    passage_total, passage_tokens, depth = passages.shape
    chunks = passage_total * passage_tokens // CHUNK
    near = chunks * 11 // 16 // BLOCK * BLOCK
    return pl.pallas_call(
        pack_body,
        out_shape=(
            pltpu.VMEM((near, CHUNK, depth), passages.dtype),
            pltpu.HBM((chunks - near, CHUNK, depth), passages.dtype),
            pltpu.SMEM((chunks + BLOCK,), jnp.int32),
            pltpu.SMEM((1,), jnp.int32),
        ),
        in_specs=[SCALARS, WHOLE],
        out_specs=(WHOLE, pl.BlockSpec(memory_space=pltpu.HBM), SCALARS, SCALARS),
        scratch_shapes=[
            pltpu.VMEM((chunks, CHUNK, depth), passages.dtype),
            pltpu.SemaphoreType.DMA((2,)),
        ],
        compiler_params=pltpu.CompilerParams(vmem_limit_bytes=KERNEL_VMEM),
        name="pack",
    )(lengths, passages)


def score_body(
    codes_ref,
    total_ref,
    near_ref,
    far_ref,
    queries_ref,
    scores_ref,
    turned_ref,
    best_ref,
    rows_ref,
    fetched_ref,
    sem,
):
    query_count, query_tokens, depth = queries_ref.shape
    passage_total = scores_ref.shape[1]
    columns = query_count * query_tokens
    width = min(columns, 512)
    fetch = pltpu.make_async_copy(far_ref, fetched_ref, sem)
    fetch.start()
    turned_ref[...] = queries_ref[...].reshape(columns, depth).T

    def block(i, running, packed_ref, first):
        rows = packed_ref[pl.ds((i - first) * BLOCK, BLOCK)].reshape(BLOCK * CHUNK, depth)
        after = []
        for w in range(columns // width):
            similarity = jnp.dot(
                rows,
                turned_ref[:, w * width : (w + 1) * width],
                preferred_element_type=jnp.float32,
            )
            top = running[w]
            for j in range(BLOCK):
                chunk = similarity[j * CHUNK : (j + 1) * CHUNK]
                code = codes_ref[i * BLOCK + j]
                kept = jnp.where((code & 1) == 1, NEGATIVE, top)
                top = jnp.maximum(kept, jnp.maximum(chunk[:SUBLANES], chunk[SUBLANES:]))
                at = lax.shift_right_logical(code, 1) * PITCH
                for k in range(width // LANES):
                    best_ref[w * (width // LANES) + k, pl.ds(at, SUBLANES), :] = top[
                        :, k * LANES : (k + 1) * LANES
                    ]
            after.append(top)
        return tuple(after)

    start = jnp.full((SUBLANES, width), NEGATIVE, jnp.float32)
    blocks = lax.div(total_ref[0] + (BLOCK - 1), BLOCK)
    turn = near_ref.shape[0] // BLOCK
    running = lax.fori_loop(
        0,
        jnp.minimum(blocks, turn),
        functools.partial(block, packed_ref=near_ref, first=0),
        (start,) * (columns // width),
    )
    fetch.wait()
    lax.fori_loop(
        turn, blocks, functools.partial(block, packed_ref=fetched_ref, first=turn), running
    )

    per = LANES // query_tokens
    for k in range(columns // LANES):
        for g in range(passage_total // SUBLANES):
            base = g * SUBLANES * PITCH
            top = best_ref[k, pl.ds(base, SUBLANES, stride=PITCH), :]
            for s in range(1, SUBLANES):
                top = jnp.maximum(top, best_ref[k, pl.ds(base + s, SUBLANES, stride=PITCH), :])
            rows_ref[g * SUBLANES : (g + 1) * SUBLANES, :] = top
        turned = rows_ref[...].T
        for j in range(per):
            scores_ref[k * per + j : k * per + j + 1, :] = jnp.sum(
                turned[j * query_tokens : (j + 1) * query_tokens], axis=0, keepdims=True
            )


def score_all(queries, near, far, codes, total, passage_total):
    query_total, query_tokens, depth = queries.shape
    tile = min(query_total, 32)
    columns = tile * query_tokens
    return pl.pallas_call(
        score_body,
        out_shape=jax.ShapeDtypeStruct((query_total, passage_total), jnp.float32),
        grid=(query_total // tile,),
        in_specs=[
            SCALARS,
            SCALARS,
            WHOLE,
            pl.BlockSpec(memory_space=pltpu.HBM),
            pl.BlockSpec((tile, query_tokens, depth), lambda q: (q, 0, 0)),
        ],
        out_specs=pl.BlockSpec((tile, passage_total), lambda q: (q, 0)),
        scratch_shapes=[
            pltpu.VMEM((depth, columns), jnp.bfloat16),
            pltpu.VMEM((columns // LANES, (passage_total + 1) * PITCH, LANES), jnp.float32),
            pltpu.VMEM((passage_total, LANES), jnp.float32),
            pltpu.VMEM(far.shape, far.dtype),
            pltpu.SemaphoreType.DMA,
        ],
        compiler_params=pltpu.CompilerParams(vmem_limit_bytes=KERNEL_VMEM),
        name="maxsim",
    )(codes, total, near, pltpu.with_memory_space_constraint(far, pltpu.HBM), queries)


def pick_body(table_ref, owner_ref, slot_ref, scores_ref, best_ref):
    owners, passages = table_ref.shape
    chunks = owner_ref.shape[1] // LANES

    def grid_of(ref):
        return jnp.concatenate(
            [ref[:, r * LANES : (r + 1) * LANES] for r in range(chunks)], axis=0
        )

    owner = grid_of(owner_ref)
    slot = grid_of(slot_ref)
    picked = jnp.zeros(owner.shape, jnp.float32)
    for o in range(owners):
        row = jnp.broadcast_to(table_ref[o : o + 1, :], owner.shape[:1] + (passages,))
        picked = jnp.where(owner == o, jnp.take_along_axis(row, slot, axis=1), picked)
    for r in range(chunks):
        scores_ref[:, r * LANES : (r + 1) * LANES] = picked[r : r + 1]

    square = (LANES, LANES)
    lower = lax.broadcasted_iota(jnp.int32, square, 0) < lax.broadcasted_iota(jnp.int32, square, 1)
    along = [jnp.broadcast_to(picked[r : r + 1], square) for r in range(chunks)]
    down = [a.T for a in along]
    place = lax.broadcasted_iota(jnp.int32, square, 0)
    kept = jnp.zeros(square, jnp.float32)
    for i in range(chunks):
        ahead = jnp.zeros(square, jnp.int32)
        for j in range(chunks):
            if j < i:
                wins = down[j] >= along[i]
            elif j > i:
                wins = down[j] > along[i]
            else:
                wins = (down[j] > along[i]) | ((down[j] == along[i]) & lower)
            ahead = ahead + wins.astype(jnp.int32)
        rank = jnp.sum(ahead, axis=0, keepdims=True)
        kept = kept + jnp.where(place == rank, along[i], 0.0)
    best_ref[...] = jnp.sum(kept.T, axis=0, keepdims=True)[:, : best_ref.shape[1]]


def pick(table, owner, slot):
    rows, candidates = slot.shape
    return pl.pallas_call(
        pick_body,
        out_shape=(
            jax.ShapeDtypeStruct((rows, candidates), jnp.float32),
            jax.ShapeDtypeStruct((rows, TOPK), jnp.float32),
        ),
        name="pick",
    )(table, owner, slot)


def shards(queries, passages, lengths, cand_owner, cand_slot):
    device_total = lax.axis_size("group") * lax.axis_size("shard")
    query_local, candidates = cand_slot.shape
    sent = jnp.broadcast_to(queries, (device_total,) + queries.shape[1:])
    everyone = lax.all_to_all(sent, AXES, split_axis=0, concat_axis=0, tiled=True)
    near, far, codes, total = pack(passages, lengths)
    scores = score_all(everyone, near, far, codes, total, passages.shape[0])
    table = lax.all_to_all(scores, AXES, split_axis=0, concat_axis=0, tiled=True)
    return pick(table, cand_owner.reshape(query_local, candidates), cand_slot)


def solution(mesh):
    placed = (
        P(AXES, None, None),
        P(AXES, None, None),
        P(AXES),
        P(AXES, None, None),
        P(AXES, None),
    )
    return jax.shard_map(
        shards,
        mesh=mesh,
        in_specs=placed,
        out_specs=(P(AXES, None), P(AXES, None)),
        check_vma=False,
    )
```

time: 44.6 us -> 38.8 us (0.87)
  blocking collectives: 27.5 us -> 9.95 us
  starting transfers between devices: 0 us -> 7.33 us
  waiting for transfers between devices: 0 us -> 3.76 us
  local copies, waits for them, and re-layouts: 0.73 us -> 4.29 us
  Pallas kernels: 15.5 us -> 12.7 us
    all_to_all x1 -> x0, blocking collectives: 17.2 us -> none  [shards(): lax.all_to_all(sent, AXES, split_axis=0, concat_axis=0, tiled=True)]
    all_to_all x0 -> x1, starting transfers between devices: none -> 7.33 us  [shards(): lax.all_to_all(sent, AXES, split_axis=0, concat_axis=0, tiled=True)]
    pallas_call x1, Pallas kernels: 13.5 us -> 7.31 us  [score_all(): pl.pallas_call(score_body, out_shape=jax.ShapeDtypeStruct((query_total, p...]
    all_to_all x0 -> x1, waiting for transfers between devices: none -> 3.76 us  [shards(): lax.all_to_all(sent, AXES, split_axis=0, concat_axis=0, tiled=True)]
    pallas_call x0 -> x1, Pallas kernels: none -> 3.38 us  [pack(): pl.pallas_call(pack_body, out_shape=(pltpu.VMEM((near, CHUNK, depth), pas...]
    unnamed x0 -> x4, local copies, waits for them, and re-layouts: none -> 2.84 us
    broadcast_in_dim x1, local copies, waits for them, and re-layouts: 0.73 us -> 1.45 us  [shards(): sent = jnp.broadcast_to(queries, (device_total,) + queries.shape[1:])]
  transfers between devices with their start and end apart: 0 -> 1, of which waited for: 0 -> 1; matrix products, arithmetic and copies ran while one was open for 0% -> 0% of each run, Pallas kernels for 0% -> 9%
where the time goes in v2:
time: 38.8 us; the launch traced here: 38.7 us
  Pallas kernels  12.7 us (33%)
  blocking collectives  9.95 us (26%)
  starting transfers between devices  7.33 us (19%)
  local copies, waits for them, and re-layouts  4.29 us (11%)
  waiting for transfers between devices  3.76 us (10%)
  between operations  0.66 us (2%)
    all_to_all x1, blocking collectives, shards(): lax.all_to_all(scores, AXES, split_axis=0, concat_axis=0, tiled=True)  9.95 us
    all_to_all x1, starting transfers between devices, shards(): lax.all_to_all(sent, AXES, split_axis=0, concat_axis=0, tiled=True)  7.33 us
    pallas_call x1, Pallas kernels, score_all(): pl.pallas_call(score_body, out_shape=jax.ShapeDtypeStruct((query_total, p...  7.31 us
    all_to_all x1, waiting for transfers between devices, shards(): lax.all_to_all(sent, AXES, split_axis=0, concat_axis=0, tiled=True)  3.76 us
    pallas_call x1, Pallas kernels, pack(): pl.pallas_call(pack_body, out_shape=(pltpu.VMEM((near, CHUNK, depth), pas...  3.38 us
    unnamed x4, local copies, waits for them, and re-layouts  2.84 us
    pallas_call x1, Pallas kernels, pick(): pl.pallas_call(pick_body, out_shape=(jax.ShapeDtypeStruct((rows, candidat...  2.01 us
    broadcast_in_dim x1, local copies, waits for them, and re-layouts, shards(): sent = jnp.broadcast_to(queries, (device_total,) + queries.shape[1:])  1.45 us
  transfers between devices with their start and end apart: 1, of which 1 were waited for; matrix products, arithmetic and copies ran while one was open for 0% of the time, Pallas kernels for 9%

profile of v2, /device:TPU:0, one launch (start us, length us, event | category | flops | bytes accessed | tf_op | source)
XLA Modules:
  0.0 38.7 jit_solution(10499662909112405897)
XLA Ops:
  0.6 1.5 %broadcast_in_dim.8 = bf16[32,32,128]{2,1,0:T(8,128)(2,1)} broadcast(bf16[32,128]{1,0:T(8,128)(2,1)} %bitcast.8), dimensions={1,2} | broadcast | bytes 270336 | tf_op jit(solution)/shard_map/broadcast_in_dim | solution.py:241
  2.1 7.3 %all-to-all-start = ((bf16[32,32,128]{2,1,0:T(8,128)(2,1)}), bf16[32,32,128]{2,1,0:T(8,128)(2,1)S(1)}, u32[]{:S(2)}, u32[]{:S(2)}) async-start(bf16[32,32,128]{2,1,0:T(8,128)(2,1)} %broadcast_in_dim.8), calls=%async_computation | async-start | bytes 524288 | tf_op jit(solution)/shard_map/all_to_all | solution.py:242
  9.4 0.0 copy-start
  9.4 2.2 %copy-done = bf16[128,128,128]{2,1,0:T(8,128)(2,1)S(1)} copy-done((bf16[128,128,128]{2,1,0:T(8,128)(2,1)S(1)}, bf16[128,128,128]{2,1,0:T(8,128)(2,1)}, u32[]{:S(2)}) %copy-start) | copy-done | bytes 4194328
  11.6 0.0 copy-start.1
  11.6 0.7 %copy-done.1 = s32[128]{0:T(128)S(1)} copy-done((s32[128]{0:T(128)S(1)}, s32[128]{0:T(128)}, u32[]{:S(2)}) %copy-start.1) | copy-done | bytes 536
  12.3 3.4 %pack.1 = (bf16[704,16,128]{2,1,0:T(8,128)(2,1)S(1)}, bf16[320,16,128]{2,1,0:T(8,128)(2,1)}, s32[1088]{0:T(1024)S(4)}, s32[1]{0:T(128)S(4)}) custom-call(s32[128]{0:T(128)S(1)} %copy-done.1, bf16[128,128,128]{2,1,0:T(8,128)(2,1)S(1)} %copy-done), custom_call_target="tpu_custom_call" | custom-call | tf_op jit(solution)/shard_map/pack/pallas_call | solution.py:67
  15.7 3.8 %all-to-all-done.queries_ref = bf16[32,32,128]{2,1,0:T(8,128)(2,1)S(1)} async-done(((bf16[32,32,128]{2,1,0:T(8,128)(2,1)}), bf16[32,32,128]{2,1,0:T(8,128)(2,1)S(1)}, u32[]{:S(2)}, u32[]{:S(2)}) %all-to-all-start) | async-done | bytes 262176 | tf_op jit(solution)/shard_map/all_to_all | solution.py:242
  19.4 7.3 %maxsim.1 = f32[32,128]{1,0:T(8,128)S(1)} custom-call(s32[1088]{0:T(1024)S(4)} %get-tuple-element.6.codes_ref, s32[1]{0:T(128)S(4)} %get-tuple-element.7.total_ref, bf16[704,16,128]{2,1,0:T(8,128)(2,1)S(1)} %get-tuple-element.8.near_ref, bf16[320,16,128]{2,1,0:T(8,128)(2,1)} %get-tuple-element.9.far_ref, bf16[32,32,128]{2,1,0:T(8,128)(2,1)S(1)} %all-to-all-done.queries_ref), custom_call_target="tpu_custom_call" | custom-call | tf_op jit(solution)/shard_map/maxsim/pallas_call | solution.py:163
  26.7 10.0 %all_to_all.16 = f32[32,1,128]{2,1,0:T(1,128)} all-to-all(f32[32,1,128]{2,1,0:T(1,128)S(1)} %bitcast.6), channel_id=1, replica_groups=mesh['group'=4,'shard'=8] {'group','shard'}, dimensions={0} | all-to-all | bytes 32768 | tf_op jit(solution)/shard_map/all_to_all | solution.py:245
  36.7 2.0 %pick.1 = (f32[1,1024]{1,0:T(1,128)}, f32[1,100]{1,0:T(1,128)}) custom-call(f32[32,128]{1,0:T(8,128)} %bitcast.7, s32[1,1024]{1,0:T(1,128)} %bitcast.9, s32[1,1024]{1,0:T(1,128)} %slot_ref.1), custom_call_target="tpu_custom_call" | custom-call | tf_op jit(solution)/shard_map/pick/pallas_call | solution.py:228
Async XLA Ops:
  2.1 17.3 %all-to-all-start = ((bf16[32,32,128]{2,1,0:T(8,128)(2,1)}), bf16[32,32,128]{2,1,0:T(8,128)(2,1)S(1)}, u32[]{:S(2)}, u32[]{:S(2)}) async-start(bf16[32,32,128]{2,1,0:T(8,128)(2,1)} %broadcast_in_dim.8), calls=%async_computation | async-start | bytes 524288 | tf_op jit(solution)/shard_map/all_to_all | solution.py:242
  9.4 2.2 %copy-start = (bf16[128,128,128]{2,1,0:T(8,128)(2,1)S(1)}, bf16[128,128,128]{2,1,0:T(8,128)(2,1)}, u32[]{:S(2)}) copy-start(bf16[128,128,128]{2,1,0:T(8,128)(2,1)} %passages_ref.1) | copy-start | bytes 12582916
  11.6 0.7 %copy-start.1 = (s32[128]{0:T(128)S(1)}, s32[128]{0:T(128)}, u32[]{:S(2)}) copy-start(s32[128]{0:T(128)} %lengths_ref.1) | copy-start | bytes 1540

commit v3 on v2

--- a/solution.py
+++ b/solution.py
@@ -12,8 +12,9 @@
 LANES = 128
 SUBLANES = 8
 PITCH = SUBLANES + 1
-CHUNK = 16
-BLOCK = 64
+CHUNK = SUBLANES
+BLOCK = 128
+TAIL = 32
 KERNEL_VMEM = 24 << 20
 AXES = ("group", "shard")
 WHOLE = pl.BlockSpec(memory_space=pltpu.VMEM)
@@ -36,9 +37,9 @@
         row = lax.broadcasted_iota(jnp.int32, (CHUNK, depth), 0)
         filled = jnp.where(row < length - last * CHUNK, tail.astype(jnp.float32), first_token)
         packed_ref[pl.ds(at + last, 1)] = filled.astype(packed_ref.dtype)[None]
-        codes_ref[at] = 2 * p + 1
+        codes_ref[at] = 2 * PITCH * p + 1
         for k in range(1, most):
-            codes_ref[at + k] = 2 * p
+            codes_ref[at + k] = 2 * PITCH * p
         return at + count
 
     total = lax.fori_loop(0, passage_total, place, jnp.int32(0), unroll=4)
@@ -52,7 +53,7 @@
         copy.start()
 
     def fill(k, carry):
-        codes_ref[total + k] = 2 * passage_total + 1
+        codes_ref[total + k] = 2 * PITCH * passage_total + 1
         return carry
 
     lax.fori_loop(0, codes_ref.shape[0] - passage_total * most, fill, 0, unroll=8)
@@ -69,7 +70,7 @@
         out_shape=(
             pltpu.VMEM((near, CHUNK, depth), passages.dtype),
             pltpu.HBM((chunks - near, CHUNK, depth), passages.dtype),
-            pltpu.SMEM((chunks + BLOCK,), jnp.int32),
+            pltpu.SMEM((chunks + TAIL,), jnp.int32),
             pltpu.SMEM((1,), jnp.int32),
         ),
         in_specs=[SCALARS, WHOLE],
@@ -104,42 +105,44 @@
     fetch.start()
     turned_ref[...] = queries_ref[...].reshape(columns, depth).T
 
-    def block(i, running, packed_ref, first):
-        rows = packed_ref[pl.ds((i - first) * BLOCK, BLOCK)].reshape(BLOCK * CHUNK, depth)
-        after = []
-        for w in range(columns // width):
-            similarity = jnp.dot(
-                rows,
-                turned_ref[:, w * width : (w + 1) * width],
-                preferred_element_type=jnp.float32,
-            )
-            top = running[w]
-            for j in range(BLOCK):
-                chunk = similarity[j * CHUNK : (j + 1) * CHUNK]
-                code = codes_ref[i * BLOCK + j]
-                kept = jnp.where((code & 1) == 1, NEGATIVE, top)
-                top = jnp.maximum(kept, jnp.maximum(chunk[:SUBLANES], chunk[SUBLANES:]))
-                at = lax.shift_right_logical(code, 1) * PITCH
-                for k in range(width // LANES):
-                    best_ref[w * (width // LANES) + k, pl.ds(at, SUBLANES), :] = top[
-                        :, k * LANES : (k + 1) * LANES
-                    ]
-            after.append(top)
-        return tuple(after)
-
-    start = jnp.full((SUBLANES, width), NEGATIVE, jnp.float32)
-    blocks = lax.div(total_ref[0] + (BLOCK - 1), BLOCK)
-    turn = near_ref.shape[0] // BLOCK
-    running = lax.fori_loop(
-        0,
-        jnp.minimum(blocks, turn),
-        functools.partial(block, packed_ref=near_ref, first=0),
-        (start,) * (columns // width),
-    )
+    def sweep(packed_ref, first, size, blocks, start, running):
+        def block(i, running):
+            base = start + i * size
+            rows = packed_ref[pl.ds(base - first, size)].reshape(size * CHUNK, depth)
+            after = []
+            for w in range(columns // width):
+                similarity = jnp.dot(
+                    rows,
+                    turned_ref[:, w * width : (w + 1) * width],
+                    preferred_element_type=jnp.float32,
+                )
+                top = running[w]
+                for j in range(size):
+                    code = codes_ref[base + j]
+                    kept = jnp.where((code & 1) == 1, NEGATIVE, top)
+                    top = jnp.maximum(kept, similarity[j * CHUNK : (j + 1) * CHUNK])
+                    at = lax.shift_right_logical(code, 1)
+                    for k in range(width // LANES):
+                        best_ref[w * (width // LANES) + k, pl.ds(at, SUBLANES), :] = top[
+                            :, k * LANES : (k + 1) * LANES
+                        ]
+                after.append(top)
+            return tuple(after)
+
+        return lax.fori_loop(0, blocks, block, running)
+
+    total = total_ref[0]
+    near = near_ref.shape[0]
+    full = lax.div(total, BLOCK)
+    rest = lax.div(total - full * BLOCK + (TAIL - 1), TAIL)
+    turn = near // BLOCK
+    inside = full < turn
+    running = (jnp.full((SUBLANES, width), NEGATIVE, jnp.float32),) * (columns // width)
+    running = sweep(near_ref, 0, BLOCK, jnp.minimum(full, turn), 0, running)
+    running = sweep(near_ref, 0, TAIL, jnp.where(inside, rest, 0), full * BLOCK, running)
     fetch.wait()
-    lax.fori_loop(
-        turn, blocks, functools.partial(block, packed_ref=fetched_ref, first=turn), running
-    )
+    running = sweep(fetched_ref, near, BLOCK, jnp.maximum(full - turn, 0), near, running)
+    sweep(fetched_ref, near, TAIL, jnp.where(inside, 0, rest), full * BLOCK, running)
 
     per = LANES // query_tokens
     for k in range(columns // LANES):
@@ -231,6 +234,8 @@
             jax.ShapeDtypeStruct((rows, candidates), jnp.float32),
             jax.ShapeDtypeStruct((rows, TOPK), jnp.float32),
         ),
+        in_specs=[WHOLE, WHOLE, WHOLE],
+        compiler_params=pltpu.CompilerParams(vmem_limit_bytes=KERNEL_VMEM),
         name="pick",
     )(table, owner, slot)
 
@@ -239,10 +244,12 @@
     device_total = lax.axis_size("group") * lax.axis_size("shard")
     query_local, candidates = cand_slot.shape
     sent = jnp.broadcast_to(queries, (device_total,) + queries.shape[1:])
+    sent = pltpu.with_memory_space_constraint(sent, pltpu.VMEM)
     everyone = lax.all_to_all(sent, AXES, split_axis=0, concat_axis=0, tiled=True)
     near, far, codes, total = pack(passages, lengths)
     scores = score_all(everyone, near, far, codes, total, passages.shape[0])
     table = lax.all_to_all(scores, AXES, split_axis=0, concat_axis=0, tiled=True)
+    table = pltpu.with_memory_space_constraint(table, pltpu.VMEM)
     return pick(table, cand_owner.reshape(query_local, candidates), cand_slot)
 
 

time: 38.8 us -> 37.5 us (0.966)
  waiting for transfers between devices: 3.76 us -> 3.21 us
  Pallas kernels: 12.7 us -> 12.3 us
  blocking collectives: 9.95 us -> 9.56 us
    pallas_call x1, Pallas kernels: 2.01 us -> 1.27 us  [pick(): pl.pallas_call(pick_body, out_shape=(jax.ShapeDtypeStruct((rows, candidat...]
    all_to_all x1, waiting for transfers between devices: 3.76 us -> 3.21 us  [shards(): lax.all_to_all(sent, AXES, split_axis=0, concat_axis=0, tiled=True)]
    pallas_call x1, Pallas kernels: 3.38 us -> 3.92 us  [pack(): pl.pallas_call(pack_body, out_shape=(pltpu.VMEM((near, CHUNK, depth), pas...]
    all_to_all x1, blocking collectives: 9.95 us -> 9.56 us  [shards(): lax.all_to_all(scores, AXES, split_axis=0, concat_axis=0, tiled=True)]
    unnamed x4 -> x8, local copies, waits for them, and re-layouts: 2.84 us -> 2.85 us
  transfers between devices with their start and end apart: 1 -> 1, of which waited for: 1 -> 1; matrix products, arithmetic and copies ran while one was open for 0% -> 0% of each run, Pallas kernels for 9% -> 10%
where the time goes in v3:
time: 37.5 us; the launch traced here: 37.3 us
  Pallas kernels  12.3 us (33%)
  blocking collectives  9.56 us (25%)
  starting transfers between devices  7.33 us (20%)
  local copies, waits for them, and re-layouts  4.28 us (11%)
  waiting for transfers between devices  3.21 us (9%)
  between operations  0.68 us (2%)
    all_to_all x1, blocking collectives, shards(): lax.all_to_all(scores, AXES, split_axis=0, concat_axis=0, tiled=True)  9.56 us
    all_to_all x1, starting transfers between devices, shards(): lax.all_to_all(sent, AXES, split_axis=0, concat_axis=0, tiled=True)  7.33 us
    pallas_call x1, Pallas kernels, score_all(): pl.pallas_call(score_body, out_shape=jax.ShapeDtypeStruct((query_total, p...  7.08 us
    pallas_call x1, Pallas kernels, pack(): pl.pallas_call(pack_body, out_shape=(pltpu.VMEM((near, CHUNK, depth), pas...  3.92 us
    all_to_all x1, waiting for transfers between devices, shards(): lax.all_to_all(sent, AXES, split_axis=0, concat_axis=0, tiled=True)  3.21 us
    unnamed x8, local copies, waits for them, and re-layouts  2.85 us
    broadcast_in_dim x1, local copies, waits for them, and re-layouts, shards(): sent = jnp.broadcast_to(queries, (device_total,) + queries.shape[1:])  1.43 us
    pallas_call x1, Pallas kernels, pick(): pl.pallas_call(pick_body, out_shape=(jax.ShapeDtypeStruct((rows, candidat...  1.27 us
  transfers between devices with their start and end apart: 1, of which 1 were waited for; matrix products, arithmetic and copies ran while one was open for 0% of the time, Pallas kernels for 10%

profile of v3, /device:TPU:0, one launch (start us, length us, event | category | flops | bytes accessed | tf_op | source)
XLA Modules:
  0.0 37.3 jit_solution(80747661685660348)
XLA Ops:
  0.6 1.4 %broadcast_in_dim.8 = bf16[32,32,128]{2,1,0:T(8,128)(2,1)} broadcast(bf16[32,128]{1,0:T(8,128)(2,1)} %bitcast.9), dimensions={1,2} | broadcast | bytes 270336 | tf_op jit(solution)/shard_map/broadcast_in_dim | solution.py:246
  2.1 7.3 %all-to-all-start = ((bf16[32,32,128]{2,1,0:T(8,128)(2,1)}), bf16[32,32,128]{2,1,0:T(8,128)(2,1)S(1)}, u32[]{:S(2)}, u32[]{:S(2)}) async-start(bf16[32,32,128]{2,1,0:T(8,128)(2,1)} %broadcast_in_dim.8), calls=%async_computation | async-start | bytes 524288 | tf_op jit(solution)/shard_map/all_to_all | solution.py:248
  9.4 0.0 copy-start
  9.4 2.2 %copy-done = bf16[128,128,128]{2,1,0:T(8,128)(2,1)S(1)} copy-done((bf16[128,128,128]{2,1,0:T(8,128)(2,1)S(1)}, bf16[128,128,128]{2,1,0:T(8,128)(2,1)}, u32[]{:S(2)}) %copy-start) | copy-done | bytes 4194328
  11.6 0.0 copy-start.3
  11.6 0.7 %copy-done.3 = s32[128]{0:T(128)S(1)} copy-done((s32[128]{0:T(128)S(1)}, s32[128]{0:T(128)}, u32[]{:S(2)}) %copy-start.3) | copy-done | bytes 536
  12.2 3.9 %pack.1 = (bf16[1408,8,128]{2,1,0:T(8,128)(2,1)S(1)}, bf16[640,8,128]{2,1,0:T(8,128)(2,1)}, s32[2080]{0:T(1024)S(4)}, s32[1]{0:T(128)S(4)}) custom-call(s32[128]{0:T(128)S(1)} %copy-done.3, bf16[128,128,128]{2,1,0:T(8,128)(2,1)S(1)} %copy-done), custom_call_target="tpu_custom_call" | custom-call | tf_op jit(solution)/shard_map/pack/pallas_call | solution.py:68
  16.2 0.0 copy-start.1
  16.2 0.0 copy-start.2
  16.2 3.2 %all-to-all-done.queries_ref = bf16[32,32,128]{2,1,0:T(8,128)(2,1)S(1)} async-done(((bf16[32,32,128]{2,1,0:T(8,128)(2,1)}), bf16[32,32,128]{2,1,0:T(8,128)(2,1)S(1)}, u32[]{:S(2)}, u32[]{:S(2)}) %all-to-all-start) | async-done | bytes 262176 | tf_op jit(solution)/shard_map/all_to_all | solution.py:248
  19.4 7.1 %maxsim.1 = f32[32,128]{1,0:T(8,128)S(1)} custom-call(s32[2080]{0:T(1024)S(4)} %get-tuple-element.6.codes_ref, s32[1]{0:T(128)S(4)} %get-tuple-element.7.total_ref, bf16[1408,8,128]{2,1,0:T(8,128)(2,1)S(1)} %get-tuple-element.8.near_ref, bf16[640,8,128]{2,1,0:T(8,128)(2,1)} %get-tuple-element.9.far_ref, bf16[32,32,128]{2,1,0:T(8,128)(2,1)S(1)} %all-to-all-done.queries_ref), custom_call_target="tpu_custom_call" | custom-call | tf_op jit(solution)/shard_map/maxsim/pallas_call | solution.py:166
  26.5 9.6 %all_to_all.16 = f32[32,1,128]{2,1,0:T(1,128)S(1)} all-to-all(f32[32,1,128]{2,1,0:T(1,128)S(1)} %bitcast.6), channel_id=1, replica_groups=mesh['group'=4,'shard'=8] {'group','shard'}, dimensions={0} | all-to-all | bytes 32768 | tf_op jit(solution)/shard_map/all_to_all | solution.py:251
  36.0 0.0 copy-done.1
  36.0 0.0 copy-done.2
  36.0 1.3 %pick.1 = (f32[1,1024]{1,0:T(1,128)}, f32[1,100]{1,0:T(1,128)}) custom-call(f32[32,128]{1,0:T(8,128)S(1)} %bitcast.7, s32[1,1024]{1,0:T(1,128)S(1)} %bitcast.8, s32[1,1024]{1,0:T(1,128)S(1)} %copy-done.2), custom_call_target="tpu_custom_call" | custom-call | tf_op jit(solution)/shard_map/pick/pallas_call | solution.py:231
Async XLA Ops:
  2.1 17.3 %all-to-all-start = ((bf16[32,32,128]{2,1,0:T(8,128)(2,1)}), bf16[32,32,128]{2,1,0:T(8,128)(2,1)S(1)}, u32[]{:S(2)}, u32[]{:S(2)}) async-start(bf16[32,32,128]{2,1,0:T(8,128)(2,1)} %broadcast_in_dim.8), calls=%async_computation | async-start | bytes 524288 | tf_op jit(solution)/shard_map/all_to_all | solution.py:248
  9.4 2.2 %copy-start = (bf16[128,128,128]{2,1,0:T(8,128)(2,1)S(1)}, bf16[128,128,128]{2,1,0:T(8,128)(2,1)}, u32[]{:S(2)}) copy-start(bf16[128,128,128]{2,1,0:T(8,128)(2,1)} %passages_ref.1) | copy-start | bytes 12582916
  11.6 0.7 %copy-start.3 = (s32[128]{0:T(128)S(1)}, s32[128]{0:T(128)}, u32[]{:S(2)}) copy-start(s32[128]{0:T(128)} %lengths_ref.1) | copy-start | bytes 1540
  16.2 19.9 %copy-start.1 = (s32[1,1024,1]{1,2,0:T(1,128)S(1)}, s32[1,1024,1]{1,2,0:T(1,128)}, u32[]{:S(2)}) copy-start(s32[1,1024,1]{1,2,0:T(1,128)} %param.8) | copy-start | bytes 12292
  16.2 19.9 %copy-start.2 = (s32[1,1024]{1,0:T(1,128)S(1)}, s32[1,1024]{1,0:T(1,128)}, u32[]{:S(2)}) copy-start(s32[1,1024]{1,0:T(1,128)} %slot_ref.1) | copy-start | bytes 12292

commit v4 on v3

--- a/solution.py
+++ b/solution.py
@@ -1,5 +1,3 @@
-import functools
-
 import jax
 import jax.numpy as jnp
 from jax import lax
@@ -13,12 +11,36 @@
 SUBLANES = 8
 PITCH = SUBLANES + 1
 CHUNK = SUBLANES
-BLOCK = 128
-TAIL = 32
+BLOCK = 256
+TAIL = 64
 KERNEL_VMEM = 24 << 20
 AXES = ("group", "shard")
 WHOLE = pl.BlockSpec(memory_space=pltpu.VMEM)
 SCALARS = pl.BlockSpec(memory_space=pltpu.SMEM)
+
+
+def spread_body(queries_ref, sent_ref):
+    half = sent_ref.shape[1]
+    parts = [queries_ref[0, h * half : (h + 1) * half] for h in range(2)]
+
+    def pair(d, carry):
+        for h in range(2):
+            sent_ref[2 * d + h] = parts[h]
+        return carry
+
+    lax.fori_loop(0, sent_ref.shape[0] // 2, pair, 0, unroll=8)
+
+
+def spread(queries, device_total):
+    _, query_tokens, depth = queries.shape
+    return pl.pallas_call(
+        spread_body,
+        out_shape=pltpu.VMEM((device_total, query_tokens // 2, depth), queries.dtype),
+        in_specs=[WHOLE],
+        out_specs=WHOLE,
+        compiler_params=pltpu.CompilerParams(vmem_limit_bytes=KERNEL_VMEM),
+        name="spread",
+    )(queries)
 
 
 def pack_body(
@@ -64,7 +86,7 @@
 def pack(passages, lengths):
     passage_total, passage_tokens, depth = passages.shape
     chunks = passage_total * passage_tokens // CHUNK
-    near = chunks * 11 // 16 // BLOCK * BLOCK
+    near = chunks * 3 // 4 // BLOCK * BLOCK
     return pl.pallas_call(
         pack_body,
         out_shape=(
@@ -90,13 +112,9 @@
     near_ref,
     far_ref,
     queries_ref,
-    scores_ref,
-    turned_ref,
-    best_ref,
-    rows_ref,
-    fetched_ref,
-    sem,
+    *rest_refs,
 ):
+    *earlier_ref, scores_ref, turned_ref, best_ref, rows_ref, fetched_ref, sem = rest_refs
     query_count, query_tokens, depth = queries_ref.shape
     passage_total = scores_ref.shape[1]
     columns = query_count * query_tokens
@@ -154,12 +172,16 @@
             rows_ref[g * SUBLANES : (g + 1) * SUBLANES, :] = top
         turned = rows_ref[...].T
         for j in range(per):
-            scores_ref[k * per + j : k * per + j + 1, :] = jnp.sum(
+            row = slice(k * per + j, k * per + j + 1)
+            here = jnp.sum(
                 turned[j * query_tokens : (j + 1) * query_tokens], axis=0, keepdims=True
             )
-
-
-def score_all(queries, near, far, codes, total, passage_total):
+            for ref in earlier_ref:
+                here = ref[row, :] + here
+            scores_ref[row, :] = here
+
+
+def score_all(queries, near, far, codes, total, passage_total, *earlier):
     query_total, query_tokens, depth = queries.shape
     tile = min(query_total, 32)
     columns = tile * query_tokens
@@ -173,7 +195,8 @@
             WHOLE,
             pl.BlockSpec(memory_space=pltpu.HBM),
             pl.BlockSpec((tile, query_tokens, depth), lambda q: (q, 0, 0)),
-        ],
+        ]
+        + [pl.BlockSpec((tile, passage_total), lambda q: (q, 0)) for _ in earlier],
         out_specs=pl.BlockSpec((tile, passage_total), lambda q: (q, 0)),
         scratch_shapes=[
             pltpu.VMEM((depth, columns), jnp.bfloat16),
@@ -184,7 +207,7 @@
         ],
         compiler_params=pltpu.CompilerParams(vmem_limit_bytes=KERNEL_VMEM),
         name="maxsim",
-    )(codes, total, near, pltpu.with_memory_space_constraint(far, pltpu.HBM), queries)
+    )(codes, total, near, pltpu.with_memory_space_constraint(far, pltpu.HBM), queries, *earlier)
 
 
 def pick_body(table_ref, owner_ref, slot_ref, scores_ref, best_ref):
@@ -243,11 +266,14 @@
 def shards(queries, passages, lengths, cand_owner, cand_slot):
     device_total = lax.axis_size("group") * lax.axis_size("shard")
     query_local, candidates = cand_slot.shape
-    sent = jnp.broadcast_to(queries, (device_total,) + queries.shape[1:])
-    sent = pltpu.with_memory_space_constraint(sent, pltpu.VMEM)
-    everyone = lax.all_to_all(sent, AXES, split_axis=0, concat_axis=0, tiled=True)
+    assert query_local == 1 and device_total % 2 == 0
+    halves = lax.all_to_all(
+        spread(queries, device_total), AXES, split_axis=0, concat_axis=0, tiled=True
+    )
     near, far, codes, total = pack(passages, lengths)
-    scores = score_all(everyone, near, far, codes, total, passages.shape[0])
+    others = lax.ppermute(halves, AXES, [(i, i ^ 1) for i in range(device_total)])
+    scores = score_all(halves, near, far, codes, total, passages.shape[0])
+    scores = score_all(others, near, far, codes, total, passages.shape[0], scores)
     table = lax.all_to_all(scores, AXES, split_axis=0, concat_axis=0, tiled=True)
     table = pltpu.with_memory_space_constraint(table, pltpu.VMEM)
     return pick(table, cand_owner.reshape(query_local, candidates), cand_slot)

time: 37.5 us -> 41 us (1.093)
  blocking collectives: 9.56 us -> 24.4 us
  starting transfers between devices: 7.33 us -> 0.3 us
  waiting for transfers between devices: 3.21 us -> 0.01 us
  local copies, waits for them, and re-layouts: 4.28 us -> 3.54 us
  Pallas kernels: 12.3 us -> 11.8 us
    all_to_all x0 -> x1, blocking collectives: none -> 15.3 us  [shards(): lax.all_to_all(spread(queries, device_total), AXES, split_axis=0, concat_...]
    all_to_all x1 -> x0, starting transfers between devices: 7.33 us -> none  [shards(): lax.all_to_all(sent, AXES, split_axis=0, concat_axis=0, tiled=True)]
    all_to_all x1 -> x0, waiting for transfers between devices: 3.21 us -> none  [shards(): lax.all_to_all(sent, AXES, split_axis=0, concat_axis=0, tiled=True)]
    broadcast_in_dim x1 -> x0, local copies, waits for them, and re-layouts: 1.43 us -> none  [shards(): sent = jnp.broadcast_to(queries, (device_total,) + queries.shape[1:])]
    unnamed x8 -> x10, local copies, waits for them, and re-layouts: 2.85 us -> 3.54 us
    all_to_all x1, blocking collectives: 9.56 us -> 9.12 us  [shards(): lax.all_to_all(scores, AXES, split_axis=0, concat_axis=0, tiled=True)]
    pallas_call x1 -> x2, Pallas kernels: 7.08 us -> 6.65 us  [score_all(): pl.pallas_call(score_body, out_shape=jax.ShapeDtypeStruct((query_total, p...]
  transfers between devices with their start and end apart: 1 -> 1, of which waited for: 1 -> 0; matrix products, arithmetic and copies ran while one was open for 0% -> 0% of each run, Pallas kernels for 10% -> 18%
where the time goes in v4:
time: 41 us; the launch traced here: 40.7 us
  blocking collectives  24.4 us (60%)
  Pallas kernels  11.8 us (29%)
  local copies, waits for them, and re-layouts  3.54 us (9%)
  between operations  0.69 us (2%)
    all_to_all x1, blocking collectives, shards(): lax.all_to_all(spread(queries, device_total), AXES, split_axis=0, concat_...  15.3 us
    all_to_all x1, blocking collectives, shards(): lax.all_to_all(scores, AXES, split_axis=0, concat_axis=0, tiled=True)  9.12 us
    pallas_call x2, Pallas kernels, score_all(): pl.pallas_call(score_body, out_shape=jax.ShapeDtypeStruct((query_total, p...  6.65 us
    pallas_call x1, Pallas kernels, pack(): pl.pallas_call(pack_body, out_shape=(pltpu.VMEM((near, CHUNK, depth), pas...  3.82 us
    unnamed x10, local copies, waits for them, and re-layouts  3.54 us
    pallas_call x1, Pallas kernels, pick(): pl.pallas_call(pick_body, out_shape=(jax.ShapeDtypeStruct((rows, candidat...  1.27 us
  transfers between devices with their start and end apart: 1, of which 0 were waited for; matrix products, arithmetic and copies ran while one was open for 0% of the time, Pallas kernels for 18%

profile of v4, /device:TPU:0, one launch (start us, length us, event | category | flops | bytes accessed | tf_op | source)
XLA Modules:
  0.0 40.7 jit_solution(818223559185661857)
XLA Ops:
  0.6 0.0 copy-start.1
  0.6 0.7 %copy-done.1 = bf16[1,32,128]{2,1,0:T(8,128)(2,1)S(1)} copy-done((bf16[1,32,128]{2,1,0:T(8,128)(2,1)S(1)}, bf16[1,32,128]{2,1,0:T(8,128)(2,1)}, u32[]{:S(2)}) %copy-start.1) | copy-done | bytes 8216
  1.4 15.3 %all_to_all.16.queries_ref = bf16[32,16,128]{2,1,0:T(8,128)(2,1)S(1)} all-to-all(bf16[32,16,128]{2,1,0:T(8,128)(2,1)S(1)} %spread.1), channel_id=1, replica_groups=mesh['group'=4,'shard'=8] {'group','shard'}, dimensions={0} | all-to-all | bytes 262144 | tf_op jit(solution)/shard_map/all_to_all | solution.py:270
  16.6 0.3 collective-permute-start
  16.9 0.0 copy-start
  16.9 2.2 %copy-done = bf16[128,128,128]{2,1,0:T(8,128)(2,1)S(1)} copy-done((bf16[128,128,128]{2,1,0:T(8,128)(2,1)S(1)}, bf16[128,128,128]{2,1,0:T(8,128)(2,1)}, u32[]{:S(2)}) %copy-start) | copy-done | bytes 4194328
  19.1 0.0 copy-start.4
  19.1 0.7 %copy-done.4 = s32[128]{0:T(128)S(1)} copy-done((s32[128]{0:T(128)S(1)}, s32[128]{0:T(128)}, u32[]{:S(2)}) %copy-start.4) | copy-done | bytes 536
  19.8 3.8 %pack.1 = (bf16[1536,8,128]{2,1,0:T(8,128)(2,1)S(1)}, bf16[512,8,128]{2,1,0:T(8,128)(2,1)}, s32[2112]{0:T(1024)S(4)}, s32[1]{0:T(128)S(4)}) custom-call(s32[128]{0:T(128)S(1)} %copy-done.4, bf16[128,128,128]{2,1,0:T(8,128)(2,1)S(1)} %copy-done), custom_call_target="tpu_custom_call" | custom-call | tf_op jit(solution)/shard_map/pack/pallas_call | solution.py:90
  23.6 0.0 copy-start.2
  23.6 0.0 copy-start.3
  23.6 3.3 %maxsim.2.rest_refs_0_ = f32[32,128]{1,0:T(8,128)S(1)} custom-call(s32[2112]{0:T(1024)S(4)} %get-tuple-element.6.codes_ref, s32[1]{0:T(128)S(4)} %get-tuple-element.7.total_ref, bf16[1536,8,128]{2,1,0:T(8,128)(2,1)S(1)} %get-tuple-element.8.near_ref, bf16[512,8,128]{2,1,0:T(8,128)(2,1)} %get-tuple-element.9.far_ref, ...), custom_call_target="tpu_custom_call" | custom-call | tf_op jit(solution)/shard_map/maxsim/pallas_call | solution.py:188
  27.0 0.0 collective-permute-done.queries_ref
  27.0 3.3 %maxsim.3 = f32[32,128]{1,0:T(8,128)S(1)} custom-call(s32[2112]{0:T(1024)S(4)} %get-tuple-element.6.codes_ref, s32[1]{0:T(128)S(4)} %get-tuple-element.7.total_ref, bf16[1536,8,128]{2,1,0:T(8,128)(2,1)S(1)} %get-tuple-element.8.near_ref, bf16[512,8,128]{2,1,0:T(8,128)(2,1)} %get-tuple-element.9.far_ref, ...), custom_call_target="tpu_custom_call" | custom-call | tf_op jit(solution)/shard_map/maxsim/pallas_call | solution.py:188
  30.3 9.1 %all_to_all.17 = f32[32,1,128]{2,1,0:T(1,128)S(1)} all-to-all(f32[32,1,128]{2,1,0:T(1,128)S(1)} %bitcast.5), channel_id=1, replica_groups=mesh['group'=4,'shard'=8] {'group','shard'}, dimensions={0} | all-to-all | bytes 32768 | tf_op jit(solution)/shard_map/all_to_all | solution.py:277
  39.4 0.0 copy-done.2
  39.4 0.0 copy-done.3
  39.5 1.3 %pick.1 = (f32[1,1024]{1,0:T(1,128)}, f32[1,100]{1,0:T(1,128)}) custom-call(f32[32,128]{1,0:T(8,128)S(1)} %bitcast.6, s32[1,1024]{1,0:T(1,128)S(1)} %bitcast.7, s32[1,1024]{1,0:T(1,128)S(1)} %copy-done.3), custom_call_target="tpu_custom_call" | custom-call | tf_op jit(solution)/shard_map/pick/pallas_call | solution.py:254
  (1 shorter events, 0.0 us)
Async XLA Ops:
  0.6 0.7 %copy-start.1 = (bf16[1,32,128]{2,1,0:T(8,128)(2,1)S(1)}, bf16[1,32,128]{2,1,0:T(8,128)(2,1)}, u32[]{:S(2)}) copy-start(bf16[1,32,128]{2,1,0:T(8,128)(2,1)} %queries_ref.1) | copy-start | bytes 24580
  16.6 10.3 %collective-permute-start = (bf16[32,16,128]{2,1,0:T(8,128)(2,1)S(1)}, bf16[32,16,128]{2,1,0:T(8,128)(2,1)S(1)}, u32[]{:S(2)}, u32[]{:S(2)}) collective-permute-start(bf16[32,16,128]{2,1,0:T(8,128)(2,1)S(1)} %all_to_all.16.queries_ref), channel_id=1, source_target_pairs={{0,1},{1,0},{2,3},{3,2},{4,5},{5,4},{6,7},{7,6},{8,9},{9,8},{10,11... | collective-permute-start | bytes 393224 | tf_op jit(solution)/shard_map/ppermute | solution.py:274
  16.9 2.2 %copy-start = (bf16[128,128,128]{2,1,0:T(8,128)(2,1)S(1)}, bf16[128,128,128]{2,1,0:T(8,128)(2,1)}, u32[]{:S(2)}) copy-start(bf16[128,128,128]{2,1,0:T(8,128)(2,1)} %passages_ref.1) | copy-start | bytes 12582916
  19.1 0.7 %copy-start.4 = (s32[128]{0:T(128)S(1)}, s32[128]{0:T(128)}, u32[]{:S(2)}) copy-start(s32[128]{0:T(128)} %lengths_ref.1) | copy-start | bytes 1540
  23.6 15.8 %copy-start.2 = (s32[1,1024,1]{1,2,0:T(1,128)S(1)}, s32[1,1024,1]{1,2,0:T(1,128)}, u32[]{:S(2)}) copy-start(s32[1,1024,1]{1,2,0:T(1,128)} %param.8) | copy-start | bytes 12292
  23.6 15.8 %copy-start.3 = (s32[1,1024]{1,0:T(1,128)S(1)}, s32[1,1024]{1,0:T(1,128)}, u32[]{:S(2)}) copy-start(s32[1,1024]{1,0:T(1,128)} %slot_ref.1) | copy-start | bytes 12292
